TPU v7x, 512 devices: a whole 4x8x8 slice. The times are simulated.
512 devices in a mesh: dp: 8 (over z_lo, core), gx: 64 (over y, x, z_hi).
Axes of the slice: x: 4, y: 8, z: 8 (z_hi: 2, z_lo: 4; z = z_hi * 4 + z_lo), core: 2. Of those that a mesh axis runs over, the one named last changes fastest.
Arguments:
- field: bfloat16 [8, 64, 32, 128, 128], P('dp', 'gx'), may hold values from -6 to 6
- cotangent: bfloat16 [8, 64, 32, 128, 128], P('dp', 'gx'), may hold values from -6 to 6
- spectral_weight: bfloat16 [512, 32, 2048], P('gx'), may hold values from -3 to 3
- pointwise_weight: bfloat16 [32, 32], replicated, may hold values from -1 to 1
Outputs:
- field_grad: bfloat16 [8, 64, 32, 128, 128], P('dp', 'gx')
- weight_grad: float32 [512, 32, 2048], P('gx', 'dp')
All inputs are finite; a program needn't handle non-finite values.
Results may differ from a plain program's by a relative error of at most 0.001.
Values sent between devices are 32-bit elements; how exact they have to be, the bound alone decides.
A program may use at most 64 MiB of HBM per device.

v0:
```python
import math

import jax
import jax.numpy as jnp
from jax import lax
from jax.sharding import PartitionSpec as P

M = 16


def kept_freqs(half_count, length):
    index_range = jnp.arange(2 * half_count, dtype=jnp.int32)
    return jnp.where(index_range < half_count, index_range, index_range + length - 2 * half_count)


def phase_tables(frequency, length):
    position = jnp.arange(length, dtype=jnp.int32)
    product = frequency[:, None] * position[None, :] % length
    angle_grid = product.astype(jnp.float32) * (2.0 * math.pi / length)
    return (jnp.cos(angle_grid), jnp.sin(angle_grid))


def rotation(cosine, sine):
    return jnp.stack([jnp.stack([cosine, -sine]), jnp.stack([sine, cosine])])


def einsum_exact(form, left, right):
    return jnp.einsum(form, left, right, precision=lax.Precision.HIGHEST)


def weight_terms(input_modes, cot_modes):
    in_real = input_modes[:, :, 0]
    in_imag = input_modes[:, :, 1]
    cot_real = cot_modes[:, :, 0]
    cot_imag = cot_modes[:, :, 1]
    grad_real = einsum_exact("skiq,skoq->qkio", in_real, cot_real) + einsum_exact(
        "skiq,skoq->qkio", in_imag, cot_imag
    )
    grad_imag = einsum_exact("skiq,skoq->qkio", in_real, cot_imag) - einsum_exact(
        "skiq,skoq->qkio", in_imag, cot_real
    )
    stacked = jnp.stack([grad_real, grad_imag], axis=2)
    return stacked.reshape(stacked.shape[0], stacked.shape[1], -1)


def on_device(field, cotangent, spectral_weight, pointwise_weight):
    planes = field.shape[1]
    channels = field.shape[2]
    length_y = field.shape[3]
    length_z = field.shape[4]
    width_x = planes * lax.axis_size("gx")
    kept_x = spectral_weight.shape[1]
    pair_local = spectral_weight.shape[0]
    cells_all = width_x * length_y * length_z
    cos_y, sin_y = phase_tables(kept_freqs(M, length_y), length_y)
    cos_z, sin_z = phase_tables(jnp.arange(M, dtype=jnp.int32), length_z)
    cos_x, sin_x = phase_tables(kept_freqs(kept_x // 2, width_x), width_x)
    forward_y = jnp.stack([cos_y, -sin_y])
    forward_z = rotation(cos_z.T, sin_z.T)
    forward_x = rotation(cos_x, sin_x)
    inverse_x = rotation(cos_x, -sin_x)
    inverse_y = rotation(cos_y, -sin_y)
    inverse_z = jnp.stack([cos_z, -sin_z])
    z_weight = jnp.where(jnp.arange(M) == 0, 1.0, 2.0).astype(jnp.float32) / cells_all
    weight_full = spectral_weight.astype(jnp.float32).reshape(
        pair_local, kept_x, 2, channels, channels
    )
    weight_real = weight_full[:, :, 0]
    weight_imag = weight_full[:, :, 1]

    def to_modes(data, mode_scale):
        values = data[0].astype(jnp.float32)
        along_y = einsum_exact("pcyz,rky->prckz", values, forward_y)
        mode_data = einsum_exact("prckz,rszm->psckm", along_y, forward_z * mode_scale)
        return mode_data.reshape(planes, 2, channels, -1)

    def along_x(plane_data):
        return einsum_exact("xrcq,rskx->kscq", plane_data, forward_x)

    input_local = to_modes(field, jnp.ones((M,), jnp.float32))
    cot_local = to_modes(cotangent, z_weight)
    input_planes, cot_planes = (
        lax.all_to_all(input_local, "gx", split_axis=3, concat_axis=0, tiled=True),
        lax.all_to_all(cot_local, "gx", split_axis=3, concat_axis=0, tiled=True),
    )
    input_modes = along_x(input_planes)
    cot_modes = along_x(cot_planes)
    cot_real = cot_modes[:, 0]
    cot_imag = cot_modes[:, 1]
    grad_real = einsum_exact("koq,qkio->kiq", cot_real, weight_real) + einsum_exact(
        "koq,qkio->kiq", cot_imag, weight_imag
    )
    grad_imag = einsum_exact("koq,qkio->kiq", cot_imag, weight_real) - einsum_exact(
        "koq,qkio->kiq", cot_real, weight_imag
    )
    grad_modes = jnp.stack([grad_real, grad_imag], axis=1)
    grad_planes = einsum_exact("krcq,rskx->xscq", grad_modes, inverse_x)
    returned = lax.all_to_all(grad_planes, "gx", split_axis=0, concat_axis=3, tiled=True)
    returned = returned.reshape(planes, 2, channels, 2 * M, M)
    along_y = einsum_exact("prckm,rsky->pscym", returned, inverse_y)
    spectral_part = einsum_exact("prcym,rmz->pcyz", along_y, inverse_z)
    linear_part = jnp.einsum(
        "pdyz,cd->pcyz", cotangent[0], pointwise_weight, preferred_element_type=jnp.float32
    )
    field_grad = (spectral_part + linear_part).astype(jnp.bfloat16)[None]
    local_terms = weight_terms(input_modes[None], cot_modes[None])
    weight_grad = lax.psum_scatter(local_terms, "dp", scatter_dimension=1, tiled=True)
    return (field_grad, weight_grad)


def solution(mesh):
    placed = (
        P("dp", "gx", None, None, None),
        P("dp", "gx", None, None, None),
        P("gx", None, None),
        P(),
    )
    return jax.shard_map(
        on_device,
        mesh=mesh,
        in_specs=placed,
        out_specs=(P("dp", "gx", None, None, None), P("gx", "dp", None)),
        check_vma=False,
    )
```

profile of v0, /device:TPU:2, one launch (start us, length us, event | category | flops | bytes accessed | tf_op | source)
XLA Modules:
  0.0 159.9 jit_solution(6841968848319310605)
XLA Ops:
  9.0 2.6 %convolution_bitcast_fusion.4 = f32[1,2,32,32,16]{3,4,2,1,0:T(8,128)S(1)} fusion(f32[2,32,32,128]{3,2,1,0:T(8,128)S(1)} %convolution_bitcast_fusion.1, f32[1,2,128,16]{2,3,0,1:T(8,128)S(1)} %get-tuple-element.23, f32[1,2,128,16]{2,3,0,1:T(8,128)S(1)} %get-tuple-element.22, f32[16]{0:T(128)S(1)} %fusion.82), kind=kOutput, calls=%fused_computation.20 | convolution fusion | flops 100679680 | bytes 1212480 | tf_op jit(solution)/shard_map/prckz,rszm->psckm/dot_general | solution.py:28
  12.3 1.2 reshape.547
  13.5 19.1 %all-to-all-start = ((f32[64,1,512]{2,1,0:T(1,128)}), f32[64,1,512]{2,1,0:T(1,128)S(1)}, u32[]{:S(2)}, u32[]{:S(2)}) async-start(f32[64,1,512]{2,1,0:T(1,128)} %reshape.547), calls=%async_computation | async-start | bytes 262144 | tf_op jit(solution)/shard_map/all_to_all | solution.py:84
  33.2 2.5 %convolution_bitcast_fusion.3 = f32[1,2,32,32,16]{3,4,2,1,0:T(8,128)S(1)} fusion(f32[2,32,32,128]{3,2,1,0:T(8,128)S(1)} %convolution_bitcast_fusion, f32[1,2,128,16]{2,3,0,1:T(8,128)S(1)} %get-tuple-element.23, f32[1,2,128,16]{2,3,0,1:T(8,128)S(1)} %get-tuple-element.22), kind=kOutput, calls=%fused_computation.19 | convolution fusion | flops 100671488 | bytes 1212416 | tf_op jit(solution)/shard_map/prckz,rszm->psckm/dot_general | solution.py:28
  36.5 1.2 reshape.551
  38.5 8.1 %all-to-all-done = f32[64,1,512]{2,1,0:T(1,128)S(1)} async-done(((f32[64,1,512]{2,1,0:T(1,128)}), f32[64,1,512]{2,1,0:T(1,128)S(1)}, u32[]{:S(2)}, u32[]{:S(2)}) %all-to-all-start) | async-done | bytes 131104 | tf_op jit(solution)/shard_map/all_to_all | solution.py:84
  46.6 7.0 %all-to-all-start.2 = ((f32[64,1,512]{2,1,0:T(1,128)}), f32[64,1,512]{2,1,0:T(1,128)S(1)}, u32[]{:S(2)}, u32[]{:S(2)}) async-start(f32[64,1,512]{2,1,0:T(1,128)} %reshape.551), calls=%async_computation.2 | async-start | bytes 262144 | tf_op jit(solution)/shard_map/all_to_all | solution.py:83
  57.2 10.4 %all-to-all-done.2 = f32[64,1,512]{2,1,0:T(1,128)S(1)} async-done(((f32[64,1,512]{2,1,0:T(1,128)}), f32[64,1,512]{2,1,0:T(1,128)S(1)}, u32[]{:S(2)}, u32[]{:S(2)}) %all-to-all-start.2) | async-done | bytes 131104 | tf_op jit(solution)/shard_map/all_to_all | solution.py:83
  70.4 2.3 %add_bitcast_fusion = (f32[8,32,1,32,32]{4,3,2,0,1:T(8,128)S(1)}, f32[8,32,1,32,32]{4,3,2,0,1:T(8,128)S(1)}) fusion(f32[8,32,32]{2,0,1:T(8,128)S(1)} %copy.55, f32[8,32,32]{2,0,1:T(8,128)S(1)} %copy.54, f32[8,32,32]{2,0,1:T(8,128)S(1)} %copy.53, f32[8,32,32]{2,0,1:T(8,128)S(1)} %copy.52), kind=kLoop, calls=%fused_computation.2 | loop fusion | flops 1572864 | bytes 2228224 | tf_op jit(solution)/shard_map/stack | solution.py:42
  72.7 4.3 %pad_maximum_fusion = f32[8,32,2,32,32]{4,3,2,0,1:T(8,128)} fusion(f32[8,32,1,32,32]{4,3,2,0,1:T(8,128)S(1)} %get-tuple-element.7, f32[8,32,1,32,32]{4,3,2,0,1:T(8,128)S(1)} %get-tuple-element.6), kind=kLoop, calls=%fused_computation | loop fusion | flops 524288 | bytes 4194304 | tf_op jit(solution)/shard_map/stack | solution.py:42
  77.1 7.5 %reshape.517 = f32[8,32,2048]{2,0,1:T(8,128)} reshape(f32[8,32,2,32,32]{4,3,2,0,1:T(8,128)} %pad_maximum_fusion) | data formatting | bytes 4194304 | tf_op jit(solution)/shard_map/reshape | solution.py:43
  85.8 4.4 %reshape.507 = bf16[8,32,2,32,32]{4,3,2,1,0:T(8,128)(2,1)} reshape(bf16[8,32,2048]{2,1,0:T(8,128)(2,1)S(1)} %copy-done.2) | data formatting | bytes 2097152 | tf_op jit(solution)/shard_map/reshape | solution.py:65
  90.9 3.2 %slice_bitcast_fusion.1 = (bf16[8,32,32,32]{3,2,1,0:T(8,128)(2,1)S(1)}, bf16[8,32,32,32]{3,2,1,0:T(8,128)(2,1)S(1)}) fusion(bf16[8,32,2,32,32]{4,3,2,1,0:T(8,128)(2,1)} %reshape.507), kind=kLoop, calls=%fused_computation.4 | loop fusion | bytes 2097152 | tf_op jit(solution)/shard_map/squeeze | solution.py:68
  95.5 3.3 %fusion.7 = f32[32,8,1,32]{3,2,1,0:T(1,128)S(1)} fusion(bf16[8,32,32,32]{3,2,1,0:T(8,128)(2,1)S(1)} %get-tuple-element.4, f32[32,32,8,1]{1,0,2,3:T(8,128)S(1)} %get-tuple-element.13), kind=kOutput, calls=%fused_computation.13 | convolution fusion | flops 3145728 | bytes 589824 | tf_op jit(solution)/shard_map/koq,qkio->kiq/dot_general | solution.py:28
  99.0 4.3 %fusion.3 = f32[32,8,1,32]{3,2,1,0:T(1,128)S(1)} fusion(bf16[8,32,32,32]{3,2,1,0:T(8,128)(2,1)S(1)} %get-tuple-element.5, f32[32,32,8,1]{1,0,2,3:T(8,128)} %get-tuple-element.12), kind=kOutput, calls=%fused_computation.9 | convolution fusion | flops 3145728 | bytes 589824 | tf_op jit(solution)/shard_map/koq,qkio->kiq/dot_general | solution.py:28
  103.3 5.7 %fusion.5 = f32[32,8,1,32]{3,2,1,0:T(1,128)} fusion(bf16[8,32,32,32]{3,2,1,0:T(8,128)(2,1)} %copy-done.1, f32[32,32,8,1]{1,0,2,3:T(8,128)} %get-tuple-element.12), kind=kOutput, calls=%fused_computation.11 | convolution fusion | flops 3145728 | bytes 589824 | tf_op jit(solution)/shard_map/koq,qkio->kiq/dot_general | solution.py:28
  110.0 4.9 %fusion.1 = f32[32,8,1,32]{3,2,1,0:T(1,128)} fusion(bf16[8,32,32,32]{3,2,1,0:T(8,128)(2,1)S(1)} %get-tuple-element.5, f32[32,32,8,1]{1,0,2,3:T(8,128)} %copy-done.6), kind=kOutput, calls=%fused_computation.7 | convolution fusion | flops 3145728 | bytes 589824 | tf_op jit(solution)/shard_map/koq,qkio->kiq/dot_general | solution.py:28
  118.4 5.4 %all-to-all-start.1 = ((f32[64,1,512]{2,1,0:T(1,128)}), f32[64,1,512]{2,1,0:T(1,128)S(1)}, u32[]{:S(2)}, u32[]{:S(2)}) async-start(f32[64,1,512]{2,1,0:T(1,128)} %reshape.549), calls=%async_computation.1 | async-start | bytes 262144 | tf_op jit(solution)/shard_map/all_to_all | solution.py:98
  124.6 13.3 %all-to-all-done.1 = f32[64,1,512]{2,1,0:T(1,128)S(1)} async-done(((f32[64,1,512]{2,1,0:T(1,128)}), f32[64,1,512]{2,1,0:T(1,128)S(1)}, u32[]{:S(2)}, u32[]{:S(2)}) %all-to-all-start.1) | async-done | bytes 131104 | tf_op jit(solution)/shard_map/all_to_all | solution.py:98
  139.9 1.9 %copy.41 = f32[64,2,32,8]{2,3,0,1:T(8,128)} copy(f32[64,2,32,8]{2,3,1,0:T(8,128)} %bitcast.234) | data formatting | bytes 262144 | tf_op jit(solution)/shard_map/all_to_all | solution.py:98
  141.8 2.1 %copy.43 = f32[2,32,32,16]{2,1,0,3:T(8,128)} copy(f32[2,32,32,16]{1,3,2,0:T(8,128)} %bitcast.237) | data formatting | bytes 262144 | tf_op jit(solution)/shard_map/reshape.10
  143.8 1.7 %convolution_bitcast_fusion.2 = f32[2,32,128,16]{2,1,3,0:T(8,128)S(1)} fusion(f32[2,32,32,16]{2,1,0,3:T(8,128)} %copy.43, f32[1,2,32,128]{3,2,1,0:T(8,128)S(1)} %copy-done.5, f32[1,2,32,128]{3,2,1,0:T(8,128)S(1)} %copy-done.4), kind=kOutput, calls=%fused_computation.18 | convolution fusion | flops 100679680 | bytes 720896 | tf_op jit(solution)/shard_map/prckm,rsky->pscym/dot_general | solution.py:28
  145.5 5.8 %fusion.9 = bf16[1,1,32,128,128]{4,3,2,1,0:T(8,128)(2,1)} fusion(f32[32,128,128]{2,0,1:T(8,128)S(1)} %fusion.15, f32[2,32,128,16]{2,1,3,0:T(8,128)S(1)} %convolution_bitcast_fusion.2, f32[1,16,128]{2,1,0:T(8,128)S(1)} %get-tuple-element.32, f32[1,16,128]{2,1,0:T(8,128)S(1)} %get-tuple-element.33), kind=kOutput, calls=%fused_computation.15 | convolution fusion | flops 202379264 | bytes 3686400 | tf_op jit(solution)/shard_map/prcym,rmz->pcyz/dot_general | solution.py:28
  151.3 1.8 %copy.57 = f32[8,4,2048]{2,1,0:T(4,128)} copy(f32[8,4,2048]{2,0,1:T(8,128)} %reduce-scatter.2.cloned.1.call-done) | data formatting | bytes 524288
  (64 shorter events, 21.7 us)
Async XLA Ops:
  7.2 1.2 copy-start
  9.0 23.7 %copy-start.3 = (bf16[1,1,32,128,128]{4,3,2,1,0:T(8,128)(2,1)S(1)}, bf16[1,1,32,128,128]{4,3,2,1,0:T(8,128)(2,1)}, u32[]{:S(2)}) copy-start(bf16[1,1,32,128,128]{4,3,2,1,0:T(8,128)(2,1)} %param.4) | copy-start | bytes 3145732
  13.5 33.0 %all-to-all-start = ((f32[64,1,512]{2,1,0:T(1,128)}), f32[64,1,512]{2,1,0:T(1,128)S(1)}, u32[]{:S(2)}, u32[]{:S(2)}) async-start(f32[64,1,512]{2,1,0:T(1,128)} %reshape.547), calls=%async_computation | async-start | bytes 262144 | tf_op jit(solution)/shard_map/all_to_all | solution.py:84
  46.6 21.0 %all-to-all-start.2 = ((f32[64,1,512]{2,1,0:T(1,128)}), f32[64,1,512]{2,1,0:T(1,128)S(1)}, u32[]{:S(2)}, u32[]{:S(2)}) async-start(f32[64,1,512]{2,1,0:T(1,128)} %reshape.551), calls=%async_computation.2 | async-start | bytes 262144 | tf_op jit(solution)/shard_map/all_to_all | solution.py:83
  53.6 97.7 %reduce-scatter.2.cloned.1.call-start = ((), (), s32[]{:S(2)}) async-start(), calls=%async_computation.4 | async-start | bytes 2359296 | tf_op jit(solution)/shard_map/reduce_scatter | solution.py:107
  84.6 1.2 copy-start.2
  94.1 1.4 copy-start.1
  94.8 0.7 copy-start.6
  115.0 8.9 %copy-start.7 = (bf16[32,32]{1,0:T(8,128)(2,1)S(1)}, bf16[32,32]{1,0:T(8,128)(2,1)}, u32[]{:S(2)}) copy-start(bf16[32,32]{1,0:T(8,128)(2,1)} %param.7) | copy-start | bytes 6148
  118.4 19.5 %all-to-all-start.1 = ((f32[64,1,512]{2,1,0:T(1,128)}), f32[64,1,512]{2,1,0:T(1,128)S(1)}, u32[]{:S(2)}, u32[]{:S(2)}) async-start(f32[64,1,512]{2,1,0:T(1,128)} %reshape.549), calls=%async_computation.1 | async-start | bytes 262144 | tf_op jit(solution)/shard_map/all_to_all | solution.py:98
  124.6 19.2 %copy-start.4 = (f32[1,2,32,128]{3,2,1,0:T(8,128)S(1)}, f32[1,2,32,128]{3,2,1,0:T(8,128)}, u32[]{:S(2)}) copy-start(f32[1,2,32,128]{3,2,1,0:T(8,128)} %get-tuple-element.18) | copy-start | bytes 98308
  124.6 19.2 %copy-start.5 = (f32[1,2,32,128]{3,2,1,0:T(8,128)S(1)}, f32[1,2,32,128]{3,2,1,0:T(8,128)}, u32[]{:S(2)}) copy-start(f32[1,2,32,128]{3,2,1,0:T(8,128)} %get-tuple-element.19) | copy-start | bytes 98308
Sparse Core Ops, SparseCore 0:
  84.7 37.2 reduce-scatter.1
where the time goes:
time: 161 us; the launch traced here: 160 us
  local copies, waits for them, and re-layouts  35.4 us (22%)
  matrix products  35.3 us (22%)
  starting transfers between devices  31.8 us (20%)
  waiting for transfers between devices  31.7 us (20%)
  between operations  14.4 us (9%)
  other arithmetic  11.4 us (7%)
    dot_general x13, matrix products, einsum_exact(): return jnp.einsum(form, left, right, precision=lax.Precision.HIGHEST)  34.5 us
    all_to_all x1, starting transfers between devices, on_device(): lax.all_to_all(cot_local, 'gx', split_axis=3, concat_axis=0, tiled=True)  19.1 us
    all_to_all x1, waiting for transfers between devices, on_device(): lax.all_to_all(grad_planes, 'gx', split_axis=0, concat_axis=3, tiled=True)  13.3 us
    all_to_all x1, waiting for transfers between devices, on_device(): lax.all_to_all(input_local, 'gx', split_axis=3, concat_axis=0, tiled=True)  10.4 us
    unnamed x23, local copies, waits for them, and re-layouts  9.78 us
    all_to_all x1, waiting for transfers between devices, on_device(): lax.all_to_all(cot_local, 'gx', split_axis=3, concat_axis=0, tiled=True)  8.09 us
    reshape x1, local copies, waits for them, and re-layouts, weight_terms(): return stacked.reshape(stacked.shape[0], stacked.shape[1], -1)  7.51 us
    all_to_all x1, starting transfers between devices, on_device(): lax.all_to_all(input_local, 'gx', split_axis=3, concat_axis=0, tiled=True)  7.02 us
  transfers between devices with their start and end apart: 4, of which 3 were waited for; matrix products, arithmetic and copies ran while one was open for 34% of the time, Pallas kernels for 0%

commit v1 on v0

v1 whole, which is shorter than its diff:
```python
import functools
import math

import jax
import jax.numpy as jnp
import ml_dtypes
import numpy as np
from jax import lax
from jax.experimental import pallas as pl
from jax.experimental.pallas import tpu as pltpu
from jax.sharding import PartitionSpec as P

MESH = pl.DeviceIdType.MESH
BF = jnp.bfloat16
F32 = jnp.float32
C = 32
M = 16
NY = NZ = 128
NX = 64
KX = 32
DP = 8
GX = 64
CELLS = NX * NY * NZ


def halves(table):
    high = table.astype(ml_dtypes.bfloat16)
    low = (table - high.astype(np.float64)).astype(ml_dtypes.bfloat16)
    return high, low


def angles(freqs, length):
    product = np.outer(freqs, np.arange(length)) % length
    return product * (2.0 * math.pi / length)


@functools.cache
def tables():
    freq_y = np.r_[0:M, NY - M : NY]
    freq_x = np.r_[0 : KX // 2, NX - KX // 2 : NX]
    freq_z = np.arange(M)
    ay, ax, az = angles(freq_y, NY), angles(freq_x, NX), angles(freq_z, NZ)

    def stack_rows(table):
        high, low = halves(table)
        return np.concatenate(
            [np.concatenate([high, high], 1), np.concatenate([low, np.zeros_like(low)], 1)], 0
        )

    def stack_three(table):
        high, low = halves(table)
        return np.concatenate([high, high, low], 1)

    fwd_y = np.concatenate(halves(np.concatenate([np.cos(ay), -np.sin(ay)])), 0)
    fwd_z = stack_rows(np.concatenate([np.cos(az), np.sin(az)]))
    fwd_x = stack_rows(np.concatenate([np.cos(ax), np.sin(ax)]))
    inv_x = stack_three(np.concatenate([np.cos(ax), np.sin(ax)]).T)
    inv_y = stack_three(np.concatenate([np.cos(ay), np.sin(ay)]).T)

    scale = np.ones((M, 2, 2, C), np.float32)
    scale[:, :, 1] = (np.where(freq_z == 0, 1.0, 2.0) / CELLS)[:, None, None]
    scale = scale.reshape(M, 128)

    wave = np.stack([np.cos(az), -np.sin(az)], 1).reshape(2, 8, 2, NZ)
    inv_z = np.zeros((2, 8, 8, 2, 8, NZ))
    for i in range(8):
        inv_z[:, i, :, :, i] = wave
    inv_z = np.concatenate(halves(inv_z.reshape(256, 1024)), 0)

    sums = np.zeros((8, 2, 8, C, 2, 8, 8, 2), np.float32)
    for q in range(8):
        for i in range(8):
            sums[q, 0, i, :, 0, i, q, 0] = 1
            sums[q, 1, i, :, 0, i, q, 1] = 1
            sums[q, 0, i, :, 1, i, q, 1] = 1
            sums[q, 1, i, :, 1, i, q, 0] = -1
    sums = sums.reshape(4096, 256).astype(ml_dtypes.bfloat16)

    spread_cot = np.zeros((2, 2, 2, C, 2, 4, C), np.float32)
    spread_in = np.zeros((8, 2, 2, 2, C, 2, 4, C), np.float32)
    for r in range(2):
        for o in range(C):
            spread_cot[:, r, 1, o, r, :, o] = 1
        for i in range(C):
            spread_in[i // 4, :, r, 0, i, r, i % 4, :] = 1
    spread_cot = spread_cot.reshape(256, 256).astype(ml_dtypes.bfloat16)
    spread_in = spread_in.reshape(8, 256, 256).astype(ml_dtypes.bfloat16)

    repeat16 = np.repeat(np.eye(C, dtype=np.float32), 16, 0).astype(ml_dtypes.bfloat16)
    small = [fwd_y, fwd_z, fwd_x, inv_x, inv_y, scale, spread_cot, repeat16]
    return small + [inv_z, sums, spread_in]


def split(value):
    high = value.astype(BF)
    return high, (value - high.astype(F32)).astype(BF)


def dot(left, right):
    return jnp.dot(left, right, preferred_element_type=F32)


def dot_nt(left, right):
    return lax.dot_general(left, right, (((1,), (1,)), ((), ())), preferred_element_type=F32)


def kernel(
    field_h, cot_h, weight_h, pw_ref,
    fwd_y, fwd_z, fwd_x, inv_x, inv_y, scale, spread_cot, repeat16,
    inv_z_h, sums_h, spread_in_h,
    out_ref, wg_ref,
    fx, cx, wv, inv_z, sums, spread_in,
    planes, send, recv, mb, wgr, prod, sb, rb, lin,
    load_sem, send_sem, recv_sem,
):
    dp = lax.axis_index("dp")
    me = lax.axis_index("gx")

    loads = []
    for n, (src, dst) in enumerate(((field_h, fx), (cot_h, cx))):
        for h in range(2):
            loads.append(pltpu.make_async_copy(
                src.at[0, 0, pl.ds(16 * h, 16)], dst.at[pl.ds(16 * h, 16)], load_sem.at[2 * n + h]
            ))
    later = [
        pltpu.make_async_copy(src, dst, load_sem.at[4 + n])
        for n, (src, dst) in enumerate(
            ((weight_h, wv), (sums_h, sums), (inv_z_h, inv_z), (spread_in_h, spread_in))
        )
    ]
    for copy in loads + later:
        copy.start()

    barrier = pltpu.get_barrier_semaphore()

    @pl.loop(1, GX)
    def _(step):
        pl.semaphore_signal(
            barrier, inc=1, device_id={"gx": lax.rem(me + step, GX)}, device_id_type=MESH
        )

    @pl.loop(1, DP)
    def _(step):
        pl.semaphore_signal(
            barrier, inc=1, device_id={"dp": lax.rem(dp + step, DP)}, device_id_type=MESH
        )

    lane = lax.broadcasted_iota(jnp.int32, (1, 128), 1)
    sign = jnp.where(lane < 64, 1.0, -1.0).astype(F32)
    odd = lax.rem(lane, 2) == 1

    for n, data in enumerate((fx, cx)):
        for h in range(2):
            loads[2 * n + h].wait()

            @pl.loop(0, 2)
            def _(step):
                for u in range(8):
                    c = 16 * h + 8 * step + u
                    along = dot(fwd_y[...], data[c])
                    planes[pl.ds(pl.multiple_of((32 * n + c) * 64, 64), 64), :] = (
                        along[:64] + along[64:]
                    )

    pl.semaphore_wait(barrier, GX - 1 + DP - 1)

    def send_copy(target):
        rows = pl.ds(pl.multiple_of(target * 8, 8), 8)
        return pltpu.make_async_remote_copy(
            src_ref=send.at[rows],
            dst_ref=recv.at[pl.ds(pl.multiple_of(me * 8, 8), 8)],
            send_sem=send_sem.at[0],
            recv_sem=recv_sem.at[0],
            device_id={"gx": target},
            device_id_type=MESH,
        )

    own = lax.div(me, 2)

    @pl.loop(0, 4)
    def _(step):
        for u in range(8):
            ky = lax.rem(own + 8 * step + u, 32)
            rows = jnp.concatenate(
                [planes[pl.ds(ky, 64, stride=64), :], planes[pl.ds(32 + ky, 64, stride=64), :]], 0
            )
            high, low = split(rows)
            modes = dot_nt(fwd_z[...], jnp.concatenate([high, low], 1))
            modes = modes[:32] + modes[32:]
            modes = (modes[:16] + sign * pltpu.roll(modes[16:], 64, 1)) * scale[...]
            send[pl.ds(pl.multiple_of(ky * 16, 16), 16), :] = modes
        for u in range(16):
            target = lax.rem(2 * own + 16 * step + u, GX)

            @pl.when(target != me)
            def _():
                send_copy(target).start()

    mine = pl.ds(pl.multiple_of(me * 8, 8), 8)
    recv[mine, :] = send[mine, :]

    pw_rows = dot(repeat16[...], pw_ref[...]).astype(BF)
    kron = dot_nt(pw_rows, repeat16[...])
    rows_i = lax.broadcasted_iota(jnp.int32, (512, 512), 0)
    cols_i = lax.broadcasted_iota(jnp.int32, (512, 512), 1)
    kron = jnp.where(lax.rem(rows_i, 16) == lax.rem(cols_i, 16), kron, 0.0).astype(BF)
    for g in range(8):
        block = cx[:, 16 * g : 16 * g + 16, :].reshape(512, 128)
        lin[:, 16 * g : 16 * g + 16, :] = dot(kron, block).reshape(32, 16, 128)

    def drain(buffer, rows, index):
        return pltpu.make_async_remote_copy(
            src_ref=buffer[0].at[rows], dst_ref=buffer[1].at[rows],
            send_sem=send_sem.at[index], recv_sem=recv_sem.at[index],
            device_id={"gx": lax.rem(me + 1, GX)}, device_id_type=MESH,
        )

    first = drain((send, recv), pl.ds(0, 504), 0)
    first.wait_recv()

    cols = []
    for q in range(8):
        high, low = split(recv[pl.ds(q, 64, stride=8), :])
        cols.append(jnp.concatenate([high, low], 0))
    modes_x = dot(fwd_x[...], jnp.concatenate(cols, 1))
    modes_x = modes_x[:64] + modes_x[64:]
    modes = []
    for q in range(8):
        part = modes_x[:, 128 * q : 128 * q + 128]
        part = part[:32] + sign * pltpu.roll(part[32:], 64, 1)
        mb[pl.ds(q, 32, stride=8), :] = part
        modes.append(part)

    def dp_copy(target):
        return pltpu.make_async_remote_copy(
            src_ref=mb.at[pl.ds(pl.multiple_of(target * 32, 32), 32)],
            dst_ref=wgr.at[pl.ds(pl.multiple_of(dp * 32, 32), 32)],
            send_sem=send_sem.at[1],
            recv_sem=recv_sem.at[1],
            device_id={"dp": target},
            device_id_type=MESH,
        )

    @pl.loop(1, DP)
    def _(step):
        dp_copy(lax.rem(dp + step, DP)).start()

    ours = pl.ds(pl.multiple_of(dp * 32, 32), 32)
    wgr[ours, :] = mb[ours, :]

    for copy in later[:2]:
        copy.wait()
    high, low = split(jnp.concatenate(modes, 0))
    spread = dot(jnp.concatenate([high, low], 1), spread_cot[...])
    for q in range(8):
        cr = spread[32 * q : 32 * q + 32, :128]
        ci = spread[32 * q : 32 * q + 32, 128:]
        for a in range(4):
            for g in range(2):
                col = 256 * a + 128 * g
                wr = wv[q, :, col : col + 128].astype(F32)
                wi = wv[q, :, 1024 + col : 1024 + col + 128].astype(F32)
                for r, value in enumerate((cr * wr + ci * wi, ci * wr - cr * wi)):
                    high, low = split(value)
                    at = 512 * q + 256 * r + 128 * g
                    prod[32 * a : 32 * a + 32, at : at + 128] = high
                    prod[128 + 32 * a : 160 + 32 * a, at : at + 128] = low
    grad = dot(prod[...], sums[...])
    grad = grad[:128] + grad[128:]
    pieces = [
        jnp.concatenate([grad[32 * a : 32 * a + 32, :128], grad[32 * a : 32 * a + 32, 128:]], 0)
        for a in range(4)
    ]
    high, low = split(jnp.concatenate(pieces, 1))
    back = dot(inv_x[...], jnp.concatenate([high, low, high], 0))
    for a in range(4):
        sb[pl.ds(a, 64, stride=4), :] = back[:, 128 * a : 128 * a + 128]

    sb3 = sb.reshape(64, 4, 128)
    rb3 = rb.reshape(64, 4, 128)

    def back_copy(target):
        return pltpu.make_async_remote_copy(
            src_ref=sb3.at[target],
            dst_ref=rb3.at[me],
            send_sem=send_sem.at[2],
            recv_sem=recv_sem.at[2],
            device_id={"gx": target},
            device_id_type=MESH,
        )

    @pl.loop(1, GX)
    def _(step):
        back_copy(lax.rem(me + step, GX)).start()

    rb3[me] = sb3[me]

    dp_drain = pltpu.make_async_remote_copy(
        src_ref=mb.at[pl.ds(0, 224)], dst_ref=wgr.at[pl.ds(0, 224)],
        send_sem=send_sem.at[1], recv_sem=recv_sem.at[1],
        device_id={"dp": lax.rem(dp + 1, DP)}, device_id_type=MESH,
    )
    later[3].wait()
    dp_drain.wait_recv()
    high, low = split(wgr[...])
    pair = jnp.concatenate([high, low], 1)
    spread = dot(pair, spread_cot[...])
    cr = spread[:, :128]
    ci = spread[:, 128:]
    for j in range(8):
        inner = dot(pair, spread_in[j])
        ir = inner[:, :128]
        ii = inner[:, 128:]
        for r, value in enumerate((ir * cr + ii * ci, ir * ci - ii * cr)):
            total = value[0:32]
            for s in range(1, 8):
                total = total + value[32 * s : 32 * s + 32]
            at = 1024 * r + 128 * j
            wg_ref[:, :, at : at + 128] = total.reshape(4, 8, 128)

    later[2].wait()
    third = drain((sb, rb), pl.ds(0, 252), 2)
    third.wait_recv()
    tops, bottoms = [], []
    for n in range(8):
        value = rb[pl.ds(n, 32, stride=8), :]
        tops.append(value)
        bottoms.append(jnp.where(odd, pltpu.roll(value, 1, 1), -pltpu.roll(value, 127, 1)))
    stacked = jnp.concatenate([jnp.concatenate(tops, 1), jnp.concatenate(bottoms, 1)], 0)
    high, low = split(stacked)
    along = dot(inv_y[...], jnp.concatenate([high, low, high], 0))
    for a in range(4):
        value = jnp.concatenate(
            [along[:, 128 * a : 128 * a + 128], along[:, 512 + 128 * a : 640 + 128 * a]], 1
        )
        high, low = split(value)
        both = jnp.concatenate([high, low], 0)
        for n in range(4):
            part = dot(both, inv_z[:256, 256 * n : 256 * n + 256])
            total = part[:128] + part[128:] + dot(high, inv_z[256:, 256 * n : 256 * n + 256])
            for u in range(2):
                c = 8 * a + 2 * n + u
                out_ref[0, 0, c] = (total[:, 128 * u : 128 * u + 128] + lin[c]).astype(BF)

    first.wait_send()
    dp_drain.wait_send()
    third.wait_send()


def on_device(field, cotangent, spectral_weight, pointwise_weight):
    consts = [jnp.asarray(table) for table in tables()]
    hbm = pl.BlockSpec(memory_space=pltpu.HBM)
    vmem = pl.BlockSpec(memory_space=pltpu.VMEM)
    field_grad, weight_grad = pl.pallas_call(
        kernel,
        out_shape=(
            jax.ShapeDtypeStruct((1, 1, C, NY, NZ), BF),
            jax.ShapeDtypeStruct((4, 8, 2 * C * C), F32),
        ),
        in_specs=[hbm, hbm, hbm, vmem] + [vmem] * 8 + [hbm] * 3,
        out_specs=(vmem, vmem),
        scratch_shapes=[
            pltpu.VMEM((C, NY, NZ), BF),
            pltpu.VMEM((C, NY, NZ), BF),
            pltpu.VMEM((8, KX, 2 * C * C), BF),
            pltpu.VMEM((512, 1024), BF),
            pltpu.VMEM((4096, 256), BF),
            pltpu.VMEM((8, 256, 256), BF),
            pltpu.VMEM((4096, 128), F32),
            pltpu.VMEM((512, 128), F32),
            pltpu.VMEM((512, 128), F32),
            pltpu.VMEM((256, 128), F32),
            pltpu.VMEM((256, 128), F32),
            pltpu.VMEM((256, 4096), BF),
            pltpu.VMEM((256, 128), F32),
            pltpu.VMEM((256, 128), F32),
            pltpu.VMEM((C, NY, NZ), F32),
            pltpu.SemaphoreType.DMA((8,)),
            pltpu.SemaphoreType.DMA((3,)),
            pltpu.SemaphoreType.DMA((3,)),
        ],
        compiler_params=pltpu.CompilerParams(
            collective_id=0, has_side_effects=True, vmem_limit_bytes=48 << 20
        ),
        cost_estimate=pl.CostEstimate(flops=10**10, bytes_accessed=10**7, transcendentals=0),
    )(field, cotangent, spectral_weight, pointwise_weight, *consts)
    return field_grad, jnp.transpose(weight_grad, (1, 0, 2))


def solution(mesh):
    placed = (
        P("dp", "gx", None, None, None),
        P("dp", "gx", None, None, None),
        P("gx", None, None),
        P(),
    )
    return jax.shard_map(
        on_device,
        mesh=mesh,
        in_specs=placed,
        out_specs=(P("dp", "gx", None, None, None), P("gx", "dp", None)),
        check_vma=False,
    )
```

time: 161 us -> 58.8 us (0.37)
  Pallas kernels: 0 us -> 43.7 us
  matrix products: 35.3 us -> 0 us
  starting transfers between devices: 31.8 us -> 0 us
  waiting for transfers between devices: 31.7 us -> 0 us
  local copies, waits for them, and re-layouts: 35.4 us -> 13.8 us
  between operations: 14.4 us -> 0.66 us
  other arithmetic: 11.4 us -> 0 us
    pallas_call x0 -> x1, Pallas kernels: none -> 43.7 us  [on_device(): pl.pallas_call(kernel, out_shape=(jax.ShapeDtypeStruct((1, 1, C, NY, NZ),...]
    dot_general x14 -> x0, matrix products: 35.3 us -> none  [the longest x13 34.5 us: einsum_exact(): return jnp.einsum(form, left, right, precision=lax.Precision.HIGHEST)]
    all_to_all x3 -> x0, waiting for transfers between devices: 31.7 us -> none  [the longest x1 13.3 us: on_device(): lax.all_to_all(grad_planes, 'gx', split_axis=0, concat_axis=3, tiled=True)]
    all_to_all x3 -> x0, starting transfers between devices: 31.6 us -> none  [the longest x1 19.1 us: on_device(): lax.all_to_all(cot_local, 'gx', split_axis=3, concat_axis=0, tiled=True)]
    reshape x4 -> x0, local copies, waits for them, and re-layouts: 12.7 us -> none  [the longest x1 7.51 us: weight_terms(): return stacked.reshape(stacked.shape[0], stacked.shape[1], -1)]
    another operation x7 -> x0, other arithmetic: 7.95 us -> none  [the longest x2 6.64 us: weight_terms(): stacked = jnp.stack([grad_real, grad_imag], axis=2)]
    unnamed x23 -> x28, local copies, waits for them, and re-layouts: 9.78 us -> 13.8 us
    squeeze x2 -> x0, local copies, waits for them, and re-layouts: 3.91 us -> none  [the longest x1 3.19 us: on_device(): weight_real = weight_full[:, :, 0]]
  transfers between devices with their start and end apart: 4 -> 0, of which waited for: 3 -> 0; matrix products, arithmetic and copies ran while one was open for 34% -> 0% of each run, Pallas kernels for 0% -> 0%
where the time goes in v1:
time: 58.8 us; the launch traced here: 58.1 us
  Pallas kernels  43.7 us (74%)
  local copies, waits for them, and re-layouts  13.8 us (23%)
  between operations  0.66 us (1%)
    pallas_call x1, Pallas kernels, on_device(): pl.pallas_call(kernel, out_shape=(jax.ShapeDtypeStruct((1, 1, C, NY, NZ),...  43.7 us
    unnamed x28, local copies, waits for them, and re-layouts  13.8 us

profile of v1, /device:TPU:2, one launch (start us, length us, event | category | flops | bytes accessed | tf_op | source)
XLA Modules:
  0.0 58.1 jit_solution(13497486176644465058)
XLA Ops:
  0.6 0.0 copy-start
  0.6 1.2 %copy-done = bf16[1,1,32,128,128]{4,3,2,1,0:T(8,128)(2,1)S(1)} copy-done((bf16[1,1,32,128,128]{4,3,2,1,0:T(8,128)(2,1)S(1)}, bf16[1,1,32,128,128]{4,3,2,1,0:T(8,128)(2,1)}, u32[]{:S(2)}) %copy-start) | copy-done | bytes 1048600
  1.9 0.0 copy-start.1
  1.9 1.2 %copy-done.1 = bf16[1,1,32,128,128]{4,3,2,1,0:T(8,128)(2,1)S(1)} copy-done((bf16[1,1,32,128,128]{4,3,2,1,0:T(8,128)(2,1)S(1)}, bf16[1,1,32,128,128]{4,3,2,1,0:T(8,128)(2,1)}, u32[]{:S(2)}) %copy-start.1) | copy-done | bytes 1048600
  3.1 0.0 copy-start.2
  3.1 1.2 %copy-done.2 = bf16[8,32,2048]{2,1,0:T(8,128)(2,1)S(1)} copy-done((bf16[8,32,2048]{2,1,0:T(8,128)(2,1)S(1)}, bf16[8,32,2048]{2,1,0:T(8,128)(2,1)}, u32[]{:S(2)}) %copy-start.2) | copy-done | bytes 1048600
  4.3 0.0 copy-start.3
  4.3 0.7 %copy-done.3 = bf16[32,32]{1,0:T(8,128)(2,1)S(1)} copy-done((bf16[32,32]{1,0:T(8,128)(2,1)S(1)}, bf16[32,32]{1,0:T(8,128)(2,1)}, u32[]{:S(2)}) %copy-start.3) | copy-done | bytes 2072
  5.0 0.0 copy-start.4
  5.0 1.2 %copy-done.4 = bf16[512,1024]{1,0:T(8,128)(2,1)S(1)} copy-done((bf16[512,1024]{1,0:T(8,128)(2,1)S(1)}, bf16[512,1024]{1,0:T(8,128)(2,1)}, u32[]{:S(2)}) %copy-start.4) | copy-done | bytes 1048600
  6.2 0.0 copy-start.5
  6.2 0.9 %copy-done.5 = bf16[512,32]{1,0:T(8,128)(2,1)S(1)} copy-done((bf16[512,32]{1,0:T(8,128)(2,1)S(1)}, bf16[512,32]{1,0:T(8,128)(2,1)}, u32[]{:S(2)}) %copy-start.5) | copy-done | bytes 32792
  7.1 0.0 copy-start.6
  7.1 0.9 %copy-done.6 = bf16[256,256]{1,0:T(8,128)(2,1)S(1)} copy-done((bf16[256,256]{1,0:T(8,128)(2,1)S(1)}, bf16[256,256]{1,0:T(8,128)(2,1)}, u32[]{:S(2)}) %copy-start.6) | copy-done | bytes 131096
  8.0 0.0 copy-start.7
  8.0 0.8 %copy-done.7 = bf16[128,192]{1,0:T(8,128)(2,1)S(1)} copy-done((bf16[128,192]{1,0:T(8,128)(2,1)S(1)}, bf16[128,192]{1,0:T(8,128)(2,1)}, u32[]{:S(2)}) %copy-start.7) | copy-done | bytes 49176
  8.9 0.8 %copy-done.8 = bf16[64,192]{1,0:T(8,128)(2,1)S(1)} copy-done((bf16[64,192]{1,0:T(8,128)(2,1)S(1)}, bf16[64,192]{1,0:T(8,128)(2,1)}, u32[]{:S(2)}) %copy-start.8) | copy-done | bytes 24600
  9.6 0.8 %copy-done.9 = bf16[128,128]{1,0:T(8,128)(2,1)S(1)} copy-done((bf16[128,128]{1,0:T(8,128)(2,1)S(1)}, bf16[128,128]{1,0:T(8,128)(2,1)}, u32[]{:S(2)}) %copy-start.9) | copy-done | bytes 32792
  10.4 0.8 %copy-done.10 = bf16[64,256]{1,0:T(8,128)(2,1)S(1)} copy-done((bf16[64,256]{1,0:T(8,128)(2,1)S(1)}, bf16[64,256]{1,0:T(8,128)(2,1)}, u32[]{:S(2)}) %copy-start.10) | copy-done | bytes 32792
  11.2 0.8 %copy-done.11 = bf16[128,128]{1,0:T(8,128)(2,1)S(1)} copy-done((bf16[128,128]{1,0:T(8,128)(2,1)S(1)}, bf16[128,128]{1,0:T(8,128)(2,1)}, u32[]{:S(2)}) %copy-start.11) | copy-done | bytes 32792
  11.9 0.7 %copy-done.12 = f32[16,128]{1,0:T(8,128)S(1)} copy-done((f32[16,128]{1,0:T(8,128)S(1)}, f32[16,128]{1,0:T(8,128)}, u32[]{:S(2)}) %copy-start.12) | copy-done | bytes 8216
  12.6 43.7 %shard_map.158 = (bf16[1,1,32,128,128]{4,3,2,1,0:T(8,128)(2,1)S(1)}, f32[4,8,2048]{2,1,0:T(8,128)S(1)}) custom-call(bf16[1,1,32,128,128]{4,3,2,1,0:T(8,128)(2,1)S(1)} %copy-done, bf16[1,1,32,128,128]{4,3,2,1,0:T(8,128)(2,1)S(1)} %copy-done.1, bf16[8,32,2048]{2,1,0:T(8,128)(2,1)S(1)} %copy-done.2, bf16[32,32]{1,0:T(8,128)(2,1)S(1)} %copy-done.3, ...), custom_call_target="tpu_custom_call" | custom-call | flops 10000000000 | bytes 10000000 | tf_op jit(solution)/shard_map/pallas_call | solution.py:354
  56.3 0.9 %copy.17 = f32[8,4,2048]{2,1,0:T(4,128)} copy(f32[8,4,2048]{2,0,1:T(8,128)S(1)} %bitcast.1) | data formatting | bytes 524288
  57.2 1.0 %copy.19 = bf16[1,1,32,128,128]{4,3,2,1,0:T(8,128)(2,1)} copy(bf16[1,1,32,128,128]{4,3,2,1,0:T(8,128)(2,1)S(1)} %get-tuple-element.10) | data formatting | bytes 2097152
  (5 shorter events, 0.0 us)
Async XLA Ops:
  0.6 1.2 %copy-start = (bf16[1,1,32,128,128]{4,3,2,1,0:T(8,128)(2,1)S(1)}, bf16[1,1,32,128,128]{4,3,2,1,0:T(8,128)(2,1)}, u32[]{:S(2)}) copy-start(bf16[1,1,32,128,128]{4,3,2,1,0:T(8,128)(2,1)} %field_h.1) | copy-start | bytes 3145732
  1.9 1.2 %copy-start.1 = (bf16[1,1,32,128,128]{4,3,2,1,0:T(8,128)(2,1)S(1)}, bf16[1,1,32,128,128]{4,3,2,1,0:T(8,128)(2,1)}, u32[]{:S(2)}) copy-start(bf16[1,1,32,128,128]{4,3,2,1,0:T(8,128)(2,1)} %cot_h.1) | copy-start | bytes 3145732
  3.1 1.2 %copy-start.2 = (bf16[8,32,2048]{2,1,0:T(8,128)(2,1)S(1)}, bf16[8,32,2048]{2,1,0:T(8,128)(2,1)}, u32[]{:S(2)}) copy-start(bf16[8,32,2048]{2,1,0:T(8,128)(2,1)} %weight_h.1) | copy-start | bytes 3145732
  4.3 0.7 %copy-start.3 = (bf16[32,32]{1,0:T(8,128)(2,1)S(1)}, bf16[32,32]{1,0:T(8,128)(2,1)}, u32[]{:S(2)}) copy-start(bf16[32,32]{1,0:T(8,128)(2,1)} %pw_ref.1) | copy-start | bytes 6148
  5.0 1.2 %copy-start.4 = (bf16[512,1024]{1,0:T(8,128)(2,1)S(1)}, bf16[512,1024]{1,0:T(8,128)(2,1)}, u32[]{:S(2)}) copy-start(bf16[512,1024]{1,0:T(8,128)(2,1)} %constant.30.clone.inv_z_h) | copy-start | bytes 3145732
  6.2 0.9 %copy-start.5 = (bf16[512,32]{1,0:T(8,128)(2,1)S(1)}, bf16[512,32]{1,0:T(8,128)(2,1)}, u32[]{:S(2)}) copy-start(bf16[512,32]{1,0:T(8,128)(2,1)} %constant.29.clone.repeat16) | copy-start | bytes 98308
  7.1 0.9 %copy-start.6 = (bf16[256,256]{1,0:T(8,128)(2,1)S(1)}, bf16[256,256]{1,0:T(8,128)(2,1)}, u32[]{:S(2)}) copy-start(bf16[256,256]{1,0:T(8,128)(2,1)} %constant.28.clone.spread_cot) | copy-start | bytes 393220
  8.0 0.8 %copy-start.7 = (bf16[128,192]{1,0:T(8,128)(2,1)S(1)}, bf16[128,192]{1,0:T(8,128)(2,1)}, u32[]{:S(2)}) copy-start(bf16[128,192]{1,0:T(8,128)(2,1)} %constant.26.clone.inv_y) | copy-start | bytes 147460
  8.9 0.8 %copy-start.8 = (bf16[64,192]{1,0:T(8,128)(2,1)S(1)}, bf16[64,192]{1,0:T(8,128)(2,1)}, u32[]{:S(2)}) copy-start(bf16[64,192]{1,0:T(8,128)(2,1)} %constant.25.clone.inv_x) | copy-start | bytes 73732
  9.6 0.8 %copy-start.9 = (bf16[128,128]{1,0:T(8,128)(2,1)S(1)}, bf16[128,128]{1,0:T(8,128)(2,1)}, u32[]{:S(2)}) copy-start(bf16[128,128]{1,0:T(8,128)(2,1)} %constant.24.clone.fwd_x) | copy-start | bytes 98308
  10.4 0.8 %copy-start.10 = (bf16[64,256]{1,0:T(8,128)(2,1)S(1)}, bf16[64,256]{1,0:T(8,128)(2,1)}, u32[]{:S(2)}) copy-start(bf16[64,256]{1,0:T(8,128)(2,1)} %constant.23.clone.fwd_z) | copy-start | bytes 98308
  11.2 0.8 %copy-start.11 = (bf16[128,128]{1,0:T(8,128)(2,1)S(1)}, bf16[128,128]{1,0:T(8,128)(2,1)}, u32[]{:S(2)}) copy-start(bf16[128,128]{1,0:T(8,128)(2,1)} %constant.22.clone.fwd_y) | copy-start | bytes 98308
  11.9 0.7 %copy-start.12 = (f32[16,128]{1,0:T(8,128)S(1)}, f32[16,128]{1,0:T(8,128)}, u32[]{:S(2)}) copy-start(f32[16,128]{1,0:T(8,128)} %constant.27.clone.scale) | copy-start | bytes 24580

commit v2 on v1

--- a/solution.py
+++ b/solution.py
@@ -57,10 +57,6 @@
     inv_x = stack_three(np.concatenate([np.cos(ax), np.sin(ax)]).T)
     inv_y = stack_three(np.concatenate([np.cos(ay), np.sin(ay)]).T)
 
-    scale = np.ones((M, 2, 2, C), np.float32)
-    scale[:, :, 1] = (np.where(freq_z == 0, 1.0, 2.0) / CELLS)[:, None, None]
-    scale = scale.reshape(M, 128)
-
     wave = np.stack([np.cos(az), -np.sin(az)], 1).reshape(2, 8, 2, NZ)
     inv_z = np.zeros((2, 8, 8, 2, 8, NZ))
     for i in range(8):
@@ -86,9 +82,13 @@
     spread_cot = spread_cot.reshape(256, 256).astype(ml_dtypes.bfloat16)
     spread_in = spread_in.reshape(8, 256, 256).astype(ml_dtypes.bfloat16)
 
-    repeat16 = np.repeat(np.eye(C, dtype=np.float32), 16, 0).astype(ml_dtypes.bfloat16)
-    small = [fwd_y, fwd_z, fwd_x, inv_x, inv_y, scale, spread_cot, repeat16]
-    return small + [inv_z, sums, spread_in]
+    def widen(table):
+        return np.pad(table, ((0, 0), (0, 256 - table.shape[1])))
+
+    small = np.concatenate(
+        [np.concatenate([fwd_y, fwd_x], 1), fwd_z, widen(inv_x), widen(inv_y), spread_cot], 0
+    )
+    return small, inv_z, sums, spread_in
 
 
 def split(value):
@@ -104,12 +104,25 @@
     return lax.dot_general(left, right, (((1,), (1,)), ((), ())), preferred_element_type=F32)
 
 
+def far_first(me, step):
+    y, x, z = lax.div(me, 8), lax.rem(lax.div(me, 2), 4), lax.rem(me, 2)
+    dz = 1 - lax.div(step, 32)
+    ky = far_pair(y, x, lax.rem(step, 32))
+    return 2 * ky + lax.rem(z + dz, 2)
+
+
+def far_pair(y, x, step):
+    m, j = lax.div(step, 4), lax.rem(step, 4)
+    half = lax.div(m + 1, 2)
+    dy = jnp.where(lax.rem(m, 2) == 0, 4 + half, 4 - half)
+    dx = jnp.where(j == 3, 0, jnp.where(j == 2, 3, 2 - j))
+    return lax.rem(y + dy, 8) * 4 + lax.rem(x + dx, 4)
+
+
 def kernel(
-    field_h, cot_h, weight_h, pw_ref,
-    fwd_y, fwd_z, fwd_x, inv_x, inv_y, scale, spread_cot, repeat16,
-    inv_z_h, sums_h, spread_in_h,
+    field_h, cot_h, weight_h, pw_h, small_h, inv_z_h, sums_h, spread_in_h,
     out_ref, wg_ref,
-    fx, cx, wv, inv_z, sums, spread_in,
+    fx, cx, wv, pw, small, inv_z, sums, spread_in,
     planes, send, recv, mb, wgr, prod, sb, rb, lin,
     load_sem, send_sem, recv_sem,
 ):
@@ -125,18 +138,25 @@
     later = [
         pltpu.make_async_copy(src, dst, load_sem.at[4 + n])
         for n, (src, dst) in enumerate(
-            ((weight_h, wv), (sums_h, sums), (inv_z_h, inv_z), (spread_in_h, spread_in))
+            ((weight_h, wv), (sums_h, sums), (inv_z_h, inv_z), (spread_in_h, spread_in), (pw_h, pw))
         )
     ]
-    for copy in loads + later:
+    table_load = pltpu.make_async_copy(small_h, small, load_sem.at[9])
+    for copy in [table_load] + loads:
         copy.start()
+    fwd_y = small.at[0:128, 0:128]
+    fwd_x = small.at[0:128, 128:256]
+    fwd_z = small.at[128:192]
+    inv_x = small.at[192:256, 0:192]
+    inv_y = small.at[256:384, 0:192]
+    spread_cot = small.at[384:640]
 
     barrier = pltpu.get_barrier_semaphore()
 
-    @pl.loop(1, GX)
+    @pl.loop(0, GX - 1)
     def _(step):
         pl.semaphore_signal(
-            barrier, inc=1, device_id={"gx": lax.rem(me + step, GX)}, device_id_type=MESH
+            barrier, inc=1, device_id={"gx": far_first(me, step)}, device_id_type=MESH
         )
 
     @pl.loop(1, DP)
@@ -148,6 +168,15 @@
     lane = lax.broadcasted_iota(jnp.int32, (1, 128), 1)
     sign = jnp.where(lane < 64, 1.0, -1.0).astype(F32)
     odd = lax.rem(lane, 2) == 1
+    kz = lax.broadcasted_iota(jnp.int32, (M, 128), 0)
+    scale = jnp.where(
+        lax.rem(lane, 64) < 32, 1.0, jnp.where(kz == 0, 1.0 / CELLS, 2.0 / CELLS)
+    ).astype(F32)
+    repeat_row = lax.div(lax.broadcasted_iota(jnp.int32, (512, C), 0), 16)
+    repeat_col = lax.broadcasted_iota(jnp.int32, (512, C), 1)
+    repeat16 = jnp.where(repeat_row == repeat_col, 1.0, 0.0).astype(BF)
+
+    table_load.wait()
 
     for n, data in enumerate((fx, cx)):
         for h in range(2):
@@ -162,7 +191,8 @@
                         along[:64] + along[64:]
                     )
 
-    pl.semaphore_wait(barrier, GX - 1 + DP - 1)
+    for copy in later:
+        copy.start()
 
     def send_copy(target):
         rows = pl.ds(pl.multiple_of(target * 8, 8), 8)
@@ -175,32 +205,31 @@
             device_id_type=MESH,
         )
 
-    own = lax.div(me, 2)
-
     @pl.loop(0, 4)
     def _(step):
         for u in range(8):
-            ky = lax.rem(own + 8 * step + u, 32)
+            ky = 8 * step + u
             rows = jnp.concatenate(
                 [planes[pl.ds(ky, 64, stride=64), :], planes[pl.ds(32 + ky, 64, stride=64), :]], 0
             )
             high, low = split(rows)
             modes = dot_nt(fwd_z[...], jnp.concatenate([high, low], 1))
             modes = modes[:32] + modes[32:]
-            modes = (modes[:16] + sign * pltpu.roll(modes[16:], 64, 1)) * scale[...]
+            modes = (modes[:16] + sign * pltpu.roll(modes[16:], 64, 1)) * scale
             send[pl.ds(pl.multiple_of(ky * 16, 16), 16), :] = modes
-        for u in range(16):
-            target = lax.rem(2 * own + 16 * step + u, GX)
-
-            @pl.when(target != me)
-            def _():
-                send_copy(target).start()
+
+    pl.semaphore_wait(barrier, GX - 1 + DP - 1)
+
+    @pl.loop(0, GX - 1)
+    def _(step):
+        send_copy(far_first(me, step)).start()
 
     mine = pl.ds(pl.multiple_of(me * 8, 8), 8)
     recv[mine, :] = send[mine, :]
 
-    pw_rows = dot(repeat16[...], pw_ref[...]).astype(BF)
-    kron = dot_nt(pw_rows, repeat16[...])
+    later[4].wait()
+    pw_rows = dot(repeat16, pw[...]).astype(BF)
+    kron = dot_nt(pw_rows, repeat16)
     rows_i = lax.broadcasted_iota(jnp.int32, (512, 512), 0)
     cols_i = lax.broadcasted_iota(jnp.int32, (512, 512), 1)
     kron = jnp.where(lax.rem(rows_i, 16) == lax.rem(cols_i, 16), kron, 0.0).astype(BF)
@@ -289,9 +318,9 @@
             device_id_type=MESH,
         )
 
-    @pl.loop(1, GX)
-    def _(step):
-        back_copy(lax.rem(me + step, GX)).start()
+    @pl.loop(0, GX - 1)
+    def _(step):
+        back_copy(far_first(me, step)).start()
 
     rb3[me] = sb3[me]
 
@@ -349,6 +378,7 @@
 
 def on_device(field, cotangent, spectral_weight, pointwise_weight):
     consts = [jnp.asarray(table) for table in tables()]
+    operands = [field, cotangent, spectral_weight, pointwise_weight, *consts]
     hbm = pl.BlockSpec(memory_space=pltpu.HBM)
     vmem = pl.BlockSpec(memory_space=pltpu.VMEM)
     field_grad, weight_grad = pl.pallas_call(
@@ -357,12 +387,14 @@
             jax.ShapeDtypeStruct((1, 1, C, NY, NZ), BF),
             jax.ShapeDtypeStruct((4, 8, 2 * C * C), F32),
         ),
-        in_specs=[hbm, hbm, hbm, vmem] + [vmem] * 8 + [hbm] * 3,
+        in_specs=[hbm] * 8,
         out_specs=(vmem, vmem),
         scratch_shapes=[
             pltpu.VMEM((C, NY, NZ), BF),
             pltpu.VMEM((C, NY, NZ), BF),
             pltpu.VMEM((8, KX, 2 * C * C), BF),
+            pltpu.VMEM((C, C), BF),
+            pltpu.VMEM((640, 256), BF),
             pltpu.VMEM((512, 1024), BF),
             pltpu.VMEM((4096, 256), BF),
             pltpu.VMEM((8, 256, 256), BF),
@@ -375,7 +407,7 @@
             pltpu.VMEM((256, 128), F32),
             pltpu.VMEM((256, 128), F32),
             pltpu.VMEM((C, NY, NZ), F32),
-            pltpu.SemaphoreType.DMA((8,)),
+            pltpu.SemaphoreType.DMA((10,)),
             pltpu.SemaphoreType.DMA((3,)),
             pltpu.SemaphoreType.DMA((3,)),
         ],
@@ -383,7 +415,7 @@
             collective_id=0, has_side_effects=True, vmem_limit_bytes=48 << 20
         ),
         cost_estimate=pl.CostEstimate(flops=10**10, bytes_accessed=10**7, transcendentals=0),
-    )(field, cotangent, spectral_weight, pointwise_weight, *consts)
+    )(*[pltpu.with_memory_space_constraint(x, pltpu.HBM) for x in operands])
     return field_grad, jnp.transpose(weight_grad, (1, 0, 2))
 
 

time: 58.8 us -> 40.8 us (0.69)
  the two profiles are of different devices: /device:TPU:2 before, /device:TPU:8 now
where the time goes in v2:
time: 40.8 us; the launch traced here: 40.7 us
  Pallas kernels  38.2 us (94%)
  local copies, waits for them, and re-layouts  1.84 us (5%)
  between operations  0.64 us (2%)
    pallas_call x1, Pallas kernels, on_device(): pl.pallas_call(kernel, out_shape=(jax.ShapeDtypeStruct((1, 1, C, NY, NZ),...  38.2 us
    unnamed x2, local copies, waits for them, and re-layouts  1.84 us

profile of v2, /device:TPU:8, one launch (start us, length us, event | category | flops | bytes accessed | tf_op | source)
XLA Modules:
  0.0 40.7 jit_solution(17622599992968538124)
XLA Ops:
  0.6 38.2 %shard_map.95 = (bf16[1,1,32,128,128]{4,3,2,1,0:T(8,128)(2,1)S(1)}, f32[4,8,2048]{2,1,0:T(8,128)S(1)}) custom-call(bf16[1,1,32,128,128]{4,3,2,1,0:T(8,128)(2,1)} %field_h.1, bf16[1,1,32,128,128]{4,3,2,1,0:T(8,128)(2,1)} %cot_h.1, bf16[8,32,2048]{2,1,0:T(8,128)(2,1)} %weight_h.1, bf16[32,32]{1,0:T(8,128)(2,1)} %pw_h.1, ...), custom_call_target="tpu_custom_call" | custom-call | flops 10000000000 | bytes 10000000 | tf_op jit(solution)/shard_map/pallas_call | solution.py:384
  38.9 0.9 %copy.10 = f32[8,4,2048]{2,1,0:T(4,128)} copy(f32[8,4,2048]{2,0,1:T(8,128)S(1)} %bitcast.1) | data formatting | bytes 524288
  39.7 1.0 %copy.12 = bf16[1,1,32,128,128]{4,3,2,1,0:T(8,128)(2,1)} copy(bf16[1,1,32,128,128]{4,3,2,1,0:T(8,128)(2,1)S(1)} %get-tuple-element.10) | data formatting | bytes 2097152

commit v3 on v2

--- a/solution.py
+++ b/solution.py
@@ -20,6 +20,7 @@
 KX = 32
 DP = 8
 GX = 64
+PLANE = 32
 CELLS = NX * NY * NZ
 
 
@@ -123,11 +124,14 @@
     field_h, cot_h, weight_h, pw_h, small_h, inv_z_h, sums_h, spread_in_h,
     out_ref, wg_ref,
     fx, cx, wv, pw, small, inv_z, sums, spread_in,
-    planes, send, recv, mb, wgr, prod, sb, rb, lin,
+    planes, zout, send, recv, mb, wgr, prod, sb, rb, lin,
     load_sem, send_sem, recv_sem,
 ):
     dp = lax.axis_index("dp")
     me = lax.axis_index("gx")
+    y, x, z = lax.div(me, 8), lax.rem(lax.div(me, 2), 4), lax.rem(me, 2)
+    across = me + 1 - 2 * z
+    place = lax.div(me, 2)
 
     loads = []
     for n, (src, dst) in enumerate(((field_h, fx), (cot_h, cx))):
@@ -153,11 +157,13 @@
 
     barrier = pltpu.get_barrier_semaphore()
 
-    @pl.loop(0, GX - 1)
+    @pl.loop(0, PLANE - 1)
     def _(step):
         pl.semaphore_signal(
-            barrier, inc=1, device_id={"gx": far_first(me, step)}, device_id_type=MESH
-        )
+            barrier, inc=1, device_id={"gx": 2 * far_pair(y, x, step) + z}, device_id_type=MESH
+        )
+
+    pl.semaphore_signal(barrier, inc=1, device_id={"gx": across}, device_id_type=MESH)
 
     @pl.loop(1, DP)
     def _(step):
@@ -194,14 +200,27 @@
     for copy in later:
         copy.start()
 
+    send4 = send.reshape(32, 2, 8, 128)
+    zout3 = zout.reshape(32, 8, 128)
+
+    def z_copy(part):
+        rows = pl.ds(8 * part, 8)
+        return pltpu.make_async_remote_copy(
+            src_ref=zout3.at[rows],
+            dst_ref=send4.at[rows, z],
+            send_sem=send_sem.at[3],
+            recv_sem=recv_sem.at[3],
+            device_id={"gx": across},
+            device_id_type=MESH,
+        )
+
     def send_copy(target):
-        rows = pl.ds(pl.multiple_of(target * 8, 8), 8)
         return pltpu.make_async_remote_copy(
-            src_ref=send.at[rows],
-            dst_ref=recv.at[pl.ds(pl.multiple_of(me * 8, 8), 8)],
+            src_ref=send.at[pl.ds(pl.multiple_of(target * 16, 16), 16)],
+            dst_ref=recv.at[pl.ds(pl.multiple_of(place * 16, 16), 16)],
             send_sem=send_sem.at[0],
             recv_sem=recv_sem.at[0],
-            device_id={"gx": target},
+            device_id={"gx": 2 * target + z},
             device_id_type=MESH,
         )
 
@@ -216,15 +235,25 @@
             modes = dot_nt(fwd_z[...], jnp.concatenate([high, low], 1))
             modes = modes[:32] + modes[32:]
             modes = (modes[:16] + sign * pltpu.roll(modes[16:], 64, 1)) * scale
-            send[pl.ds(pl.multiple_of(ky * 16, 16), 16), :] = modes
-
-    pl.semaphore_wait(barrier, GX - 1 + DP - 1)
-
-    @pl.loop(0, GX - 1)
-    def _(step):
-        send_copy(far_first(me, step)).start()
-
-    mine = pl.ds(pl.multiple_of(me * 8, 8), 8)
+            send[pl.ds(pl.multiple_of(ky * 16 + 8 * z, 8), 8), :] = jnp.where(
+                z == 0, modes[:8], modes[8:]
+            )
+            zout[pl.ds(pl.multiple_of(ky * 8, 8), 8), :] = jnp.where(z == 0, modes[8:], modes[:8])
+
+    pl.semaphore_wait(barrier, PLANE + DP - 1)
+    for part in range(4):
+        z_copy(part).start()
+
+    pltpu.make_async_remote_copy(
+        src_ref=zout3, dst_ref=send4.at[:, 1 - z], send_sem=send_sem.at[3], recv_sem=recv_sem.at[3],
+        device_id={"gx": across}, device_id_type=MESH,
+    ).wait_recv()
+
+    @pl.loop(0, PLANE - 1)
+    def _(step):
+        send_copy(far_pair(y, x, step)).start()
+
+    mine = pl.ds(pl.multiple_of(place * 16, 16), 16)
     recv[mine, :] = send[mine, :]
 
     later[4].wait()
@@ -241,10 +270,11 @@
         return pltpu.make_async_remote_copy(
             src_ref=buffer[0].at[rows], dst_ref=buffer[1].at[rows],
             send_sem=send_sem.at[index], recv_sem=recv_sem.at[index],
-            device_id={"gx": lax.rem(me + 1, GX)}, device_id_type=MESH,
-        )
-
-    first = drain((send, recv), pl.ds(0, 504), 0)
+            device_id={"gx": across}, device_id_type=MESH,
+        )
+
+    zero = drain((zout, recv), pl.ds(0, 256), 3)
+    first = drain((send, recv), pl.ds(0, 496), 0)
     first.wait_recv()
 
     cols = []
@@ -371,6 +401,7 @@
                 c = 8 * a + 2 * n + u
                 out_ref[0, 0, c] = (total[:, 128 * u : 128 * u + 128] + lin[c]).astype(BF)
 
+    zero.wait_send()
     first.wait_send()
     dp_drain.wait_send()
     third.wait_send()
@@ -399,6 +430,7 @@
             pltpu.VMEM((4096, 256), BF),
             pltpu.VMEM((8, 256, 256), BF),
             pltpu.VMEM((4096, 128), F32),
+            pltpu.VMEM((256, 128), F32),
             pltpu.VMEM((512, 128), F32),
             pltpu.VMEM((512, 128), F32),
             pltpu.VMEM((256, 128), F32),
@@ -408,8 +440,8 @@
             pltpu.VMEM((256, 128), F32),
             pltpu.VMEM((C, NY, NZ), F32),
             pltpu.SemaphoreType.DMA((10,)),
-            pltpu.SemaphoreType.DMA((3,)),
-            pltpu.SemaphoreType.DMA((3,)),
+            pltpu.SemaphoreType.DMA((4,)),
+            pltpu.SemaphoreType.DMA((4,)),
         ],
         compiler_params=pltpu.CompilerParams(
             collective_id=0, has_side_effects=True, vmem_limit_bytes=48 << 20

time: 40.8 us -> 44.5 us (1.091)
  the two profiles are of different devices: /device:TPU:8 before, /device:TPU:1 now
where the time goes in v3:
time: 44.5 us; the launch traced here: 44.4 us
  Pallas kernels  41.9 us (94%)
  local copies, waits for them, and re-layouts  1.84 us (4%)
  between operations  0.64 us (1%)
    pallas_call x1, Pallas kernels, on_device(): pl.pallas_call(kernel, out_shape=(jax.ShapeDtypeStruct((1, 1, C, NY, NZ),...  41.9 us
    unnamed x2, local copies, waits for them, and re-layouts  1.84 us

profile of v3, /device:TPU:1, one launch (start us, length us, event | category | flops | bytes accessed | tf_op | source)
XLA Modules:
  0.0 44.4 jit_solution(2524332470807892381)
XLA Ops:
  0.6 41.9 %shard_map.95 = (bf16[1,1,32,128,128]{4,3,2,1,0:T(8,128)(2,1)S(1)}, f32[4,8,2048]{2,1,0:T(8,128)S(1)}) custom-call(bf16[1,1,32,128,128]{4,3,2,1,0:T(8,128)(2,1)} %field_h.1, bf16[1,1,32,128,128]{4,3,2,1,0:T(8,128)(2,1)} %cot_h.1, bf16[8,32,2048]{2,1,0:T(8,128)(2,1)} %weight_h.1, bf16[32,32]{1,0:T(8,128)(2,1)} %pw_h.1, ...), custom_call_target="tpu_custom_call" | custom-call | flops 10000000000 | bytes 10000000 | tf_op jit(solution)/shard_map/pallas_call | solution.py:415
  42.6 0.9 %copy.10 = f32[8,4,2048]{2,1,0:T(4,128)} copy(f32[8,4,2048]{2,0,1:T(8,128)S(1)} %bitcast.1) | data formatting | bytes 524288
  43.4 1.0 %copy.12 = bf16[1,1,32,128,128]{4,3,2,1,0:T(8,128)(2,1)} copy(bf16[1,1,32,128,128]{4,3,2,1,0:T(8,128)(2,1)S(1)} %get-tuple-element.10) | data formatting | bytes 2097152

commit v4 on v2

--- a/solution.py
+++ b/solution.py
@@ -121,9 +121,9 @@
 
 def kernel(
     field_h, cot_h, weight_h, pw_h, small_h, inv_z_h, sums_h, spread_in_h,
-    out_ref, wg_ref,
-    fx, cx, wv, pw, small, inv_z, sums, spread_in,
-    planes, send, recv, mb, wgr, prod, sb, rb, lin,
+    back_ref, lin, wg_ref, inv_z, inv_y_ref,
+    fx, cx, wv, pw, small, sums, spread_in,
+    planes, send, recv, mb, wgr, prod, sb, rb, wgs,
     load_sem, send_sem, recv_sem,
 ):
     dp = lax.axis_index("dp")
@@ -345,19 +345,35 @@
             for s in range(1, 8):
                 total = total + value[32 * s : 32 * s + 32]
             at = 1024 * r + 128 * j
-            wg_ref[:, :, at : at + 128] = total.reshape(4, 8, 128)
-
+            wgs[at // 4 : at // 4 + 32, :] = total
+    for q in range(8):
+        for n in range(16):
+            wg_ref[q, :, 128 * n : 128 * n + 128] = wgs[pl.ds(32 * n + q, 4, stride=8), :]
+
+    inv_y_ref[...] = small[256:384, 0:192]
     later[2].wait()
     third = drain((sb, rb), pl.ds(0, 252), 2)
     third.wait_recv()
+    back_ref[...] = rb[...]
+
+    first.wait_send()
+    dp_drain.wait_send()
+    third.wait_send()
+
+
+def finish_kernel(back_ref, lin, wg_ref, inv_z, inv_y, out_h, wg_h, out, sem):
+    weights = pltpu.make_async_copy(wg_ref, wg_h, sem.at[4])
+    weights.start()
+    odd = lax.rem(lax.broadcasted_iota(jnp.int32, (1, 128), 1), 2) == 1
     tops, bottoms = [], []
     for n in range(8):
-        value = rb[pl.ds(n, 32, stride=8), :]
+        value = back_ref[pl.ds(n, 32, stride=8), :]
         tops.append(value)
         bottoms.append(jnp.where(odd, pltpu.roll(value, 1, 1), -pltpu.roll(value, 127, 1)))
     stacked = jnp.concatenate([jnp.concatenate(tops, 1), jnp.concatenate(bottoms, 1)], 0)
     high, low = split(stacked)
     along = dot(inv_y[...], jnp.concatenate([high, low, high], 0))
+    stores = []
     for a in range(4):
         value = jnp.concatenate(
             [along[:, 128 * a : 128 * a + 128], along[:, 512 + 128 * a : 640 + 128 * a]], 1
@@ -369,11 +385,12 @@
             total = part[:128] + part[128:] + dot(high, inv_z[256:, 256 * n : 256 * n + 256])
             for u in range(2):
                 c = 8 * a + 2 * n + u
-                out_ref[0, 0, c] = (total[:, 128 * u : 128 * u + 128] + lin[c]).astype(BF)
-
-    first.wait_send()
-    dp_drain.wait_send()
-    third.wait_send()
+                out[c] = (total[:, 128 * u : 128 * u + 128] + lin[c]).astype(BF)
+        rows = pl.ds(8 * a, 8)
+        stores.append(pltpu.make_async_copy(out.at[rows], out_h.at[0, 0, rows], sem.at[a]))
+        stores[-1].start()
+    for copy in stores + [weights]:
+        copy.wait()
 
 
 def on_device(field, cotangent, spectral_weight, pointwise_weight):
@@ -381,21 +398,23 @@
     operands = [field, cotangent, spectral_weight, pointwise_weight, *consts]
     hbm = pl.BlockSpec(memory_space=pltpu.HBM)
     vmem = pl.BlockSpec(memory_space=pltpu.VMEM)
-    field_grad, weight_grad = pl.pallas_call(
+    middle = pl.pallas_call(
         kernel,
         out_shape=(
-            jax.ShapeDtypeStruct((1, 1, C, NY, NZ), BF),
-            jax.ShapeDtypeStruct((4, 8, 2 * C * C), F32),
+            jax.ShapeDtypeStruct((256, 128), F32),
+            jax.ShapeDtypeStruct((C, NY, NZ), F32),
+            jax.ShapeDtypeStruct((8, 4, 2 * C * C), F32),
+            jax.ShapeDtypeStruct((512, 1024), BF),
+            jax.ShapeDtypeStruct((128, 192), BF),
         ),
         in_specs=[hbm] * 8,
-        out_specs=(vmem, vmem),
+        out_specs=(vmem,) * 5,
         scratch_shapes=[
             pltpu.VMEM((C, NY, NZ), BF),
             pltpu.VMEM((C, NY, NZ), BF),
             pltpu.VMEM((8, KX, 2 * C * C), BF),
             pltpu.VMEM((C, C), BF),
             pltpu.VMEM((640, 256), BF),
-            pltpu.VMEM((512, 1024), BF),
             pltpu.VMEM((4096, 256), BF),
             pltpu.VMEM((8, 256, 256), BF),
             pltpu.VMEM((4096, 128), F32),
@@ -406,17 +425,28 @@
             pltpu.VMEM((256, 4096), BF),
             pltpu.VMEM((256, 128), F32),
             pltpu.VMEM((256, 128), F32),
-            pltpu.VMEM((C, NY, NZ), F32),
+            pltpu.VMEM((512, 128), F32),
             pltpu.SemaphoreType.DMA((10,)),
             pltpu.SemaphoreType.DMA((3,)),
             pltpu.SemaphoreType.DMA((3,)),
         ],
         compiler_params=pltpu.CompilerParams(
-            collective_id=0, has_side_effects=True, vmem_limit_bytes=48 << 20
+            collective_id=0, has_side_effects=True, vmem_limit_bytes=40 << 20
         ),
         cost_estimate=pl.CostEstimate(flops=10**10, bytes_accessed=10**7, transcendentals=0),
     )(*[pltpu.with_memory_space_constraint(x, pltpu.HBM) for x in operands])
-    return field_grad, jnp.transpose(weight_grad, (1, 0, 2))
+    return pl.pallas_call(
+        finish_kernel,
+        out_shape=(
+            jax.ShapeDtypeStruct((1, 1, C, NY, NZ), BF),
+            jax.ShapeDtypeStruct((8, 4, 2 * C * C), F32),
+        ),
+        in_specs=[vmem] * 5,
+        out_specs=(hbm, hbm),
+        scratch_shapes=[pltpu.VMEM((C, NY, NZ), BF), pltpu.SemaphoreType.DMA((5,))],
+        compiler_params=pltpu.CompilerParams(vmem_limit_bytes=12 << 20),
+        cost_estimate=pl.CostEstimate(flops=10**9, bytes_accessed=10**6, transcendentals=0),
+    )(*middle)
 
 
 def solution(mesh):

time: 40.8 us -> 39.6 us (0.971)
  the two profiles are of different devices: /device:TPU:8 before, /device:TPU:2 now
where the time goes in v4:
time: 39.6 us; the launch traced here: 39.5 us
  Pallas kernels  38.8 us (98%)
  between operations  0.64 us (2%)
    pallas_call x1, Pallas kernels, on_device(): pl.pallas_call(kernel, out_shape=(jax.ShapeDtypeStruct((256, 128), F32),...  36.9 us
    pallas_call x1, Pallas kernels, on_device(): pl.pallas_call(finish_kernel, out_shape=(jax.ShapeDtypeStruct((1, 1, C, N...  1.97 us

profile of v4, /device:TPU:2, one launch (start us, length us, event | category | flops | bytes accessed | tf_op | source)
XLA Modules:
  0.0 39.5 jit_solution(8471289622237298949)
XLA Ops:
  0.6 36.9 %shard_map.95 = (f32[256,128]{1,0:T(8,128)S(1)}, f32[32,128,128]{2,1,0:T(8,128)S(1)}, f32[8,4,2048]{2,1,0:T(4,128)S(1)}, bf16[512,1024]{1,0:T(8,128)(2,1)S(1)}, bf16[128,192]{1,0:T(8,128)(2,1)S(1)}) custom-call(bf16[1,1,32,128,128]{4,3,2,1,0:T(8,128)(2,1)} %field_h.1, bf16[1,1,32,128,128]{4,3,2,1,0:T(8,128)(2,1)} %cot_h.1, bf16[8,32,2048]{2,1,0:T(8,128)(2,1)} %weight_h.1, ...), custom_call_target="tpu_custom_call" | custom-call | flops 10000000000 | bytes 10000000 | tf_op jit(solution)/shard_map/pallas_call | solution.py:401
  37.5 2.0 %shard_map.96 = (bf16[1,1,32,128,128]{4,3,2,1,0:T(8,128)(2,1)}, f32[8,4,2048]{2,1,0:T(4,128)}) custom-call(f32[256,128]{1,0:T(8,128)S(1)} %get-tuple-element.7.back_ref, f32[32,128,128]{2,1,0:T(8,128)S(1)} %get-tuple-element.8.lin, f32[8,4,2048]{2,1,0:T(4,128)S(1)} %get-tuple-element.9.wg_ref, bf16[512,1024]{1,0:T(8,128)(2,1)S(1)} %get-tuple-element.10.inv_z, ...), custom_call_target="tpu_custom_call" | custom-call | flops 1000000000 | bytes 1000000 | tf_op jit(solution)/shard_map/pallas_call | solution.py:438

commit v5 on v4

--- a/solution.py
+++ b/solution.py
@@ -54,23 +54,20 @@
     fwd_y = np.concatenate(halves(np.concatenate([np.cos(ay), -np.sin(ay)])), 0)
     fwd_z = stack_rows(np.concatenate([np.cos(az), np.sin(az)]))
     fwd_x = stack_rows(np.concatenate([np.cos(ax), np.sin(ax)]))
-    inv_x = stack_three(np.concatenate([np.cos(ax), np.sin(ax)]).T)
+    inv_x = np.zeros((4, NX, 2, 4, KX))
+    for a in range(4):
+        inv_x[a, :, 0, a] = np.cos(ax).T
+        inv_x[a, :, 1, a] = np.sin(ax).T
+    inv_x = np.concatenate(halves(inv_x.reshape(256, 256)), 0)
     inv_y = stack_three(np.concatenate([np.cos(ay), np.sin(ay)]).T)
 
     wave = np.stack([np.cos(az), -np.sin(az)], 1).reshape(2, 8, 2, NZ)
-    inv_z = np.zeros((2, 8, 8, 2, 8, NZ))
+    inv_z = np.zeros((2, 8, 2, 8, 8, NZ))
     for i in range(8):
-        inv_z[:, i, :, :, i] = wave
+        inv_z[:, :, :, i, i] = wave
     inv_z = np.concatenate(halves(inv_z.reshape(256, 1024)), 0)
 
-    sums = np.zeros((8, 2, 8, C, 2, 8, 8, 2), np.float32)
-    for q in range(8):
-        for i in range(8):
-            sums[q, 0, i, :, 0, i, q, 0] = 1
-            sums[q, 1, i, :, 0, i, q, 1] = 1
-            sums[q, 0, i, :, 1, i, q, 1] = 1
-            sums[q, 1, i, :, 1, i, q, 0] = -1
-    sums = sums.reshape(4096, 256).astype(ml_dtypes.bfloat16)
+    sums = np.repeat(np.eye(8), C, 1).astype(ml_dtypes.bfloat16)
 
     spread_cot = np.zeros((2, 2, 2, C, 2, 4, C), np.float32)
     spread_in = np.zeros((8, 2, 2, 2, C, 2, 4, C), np.float32)
@@ -86,9 +83,9 @@
         return np.pad(table, ((0, 0), (0, 256 - table.shape[1])))
 
     small = np.concatenate(
-        [np.concatenate([fwd_y, fwd_x], 1), fwd_z, widen(inv_x), widen(inv_y), spread_cot], 0
+        [np.concatenate([fwd_y, fwd_x], 1), fwd_z, widen(inv_y), spread_cot, inv_x, sums], 0
     )
-    return small, inv_z, sums, spread_in
+    return small, inv_z, spread_in
 
 
 def split(value):
@@ -120,9 +117,9 @@
 
 
 def kernel(
-    field_h, cot_h, weight_h, pw_h, small_h, inv_z_h, sums_h, spread_in_h,
+    field_h, cot_h, weight_h, pw_h, small_h, inv_z_h, spread_in_h,
     back_ref, lin, wg_ref, inv_z, inv_y_ref,
-    fx, cx, wv, pw, small, sums, spread_in,
+    fx, cx, wv, pw, small, spread_in,
     planes, send, recv, mb, wgr, prod, sb, rb, wgs,
     load_sem, send_sem, recv_sem,
 ):
@@ -138,18 +135,18 @@
     later = [
         pltpu.make_async_copy(src, dst, load_sem.at[4 + n])
         for n, (src, dst) in enumerate(
-            ((weight_h, wv), (sums_h, sums), (inv_z_h, inv_z), (spread_in_h, spread_in), (pw_h, pw))
+            ((weight_h, wv), (inv_z_h, inv_z), (spread_in_h, spread_in), (pw_h, pw))
         )
     ]
-    table_load = pltpu.make_async_copy(small_h, small, load_sem.at[9])
+    table_load = pltpu.make_async_copy(small_h, small, load_sem.at[8])
     for copy in [table_load] + loads:
         copy.start()
     fwd_y = small.at[0:128, 0:128]
     fwd_x = small.at[0:128, 128:256]
     fwd_z = small.at[128:192]
-    inv_x = small.at[192:256, 0:192]
-    inv_y = small.at[256:384, 0:192]
-    spread_cot = small.at[384:640]
+    spread_cot = small.at[320:576]
+    inv_x = small.at[576:1088]
+    sums = small.at[1088:1096]
 
     barrier = pltpu.get_barrier_semaphore()
 
@@ -167,7 +164,6 @@
 
     lane = lax.broadcasted_iota(jnp.int32, (1, 128), 1)
     sign = jnp.where(lane < 64, 1.0, -1.0).astype(F32)
-    odd = lax.rem(lane, 2) == 1
     kz = lax.broadcasted_iota(jnp.int32, (M, 128), 0)
     scale = jnp.where(
         lax.rem(lane, 64) < 32, 1.0, jnp.where(kz == 0, 1.0 / CELLS, 2.0 / CELLS)
@@ -227,7 +223,7 @@
     mine = pl.ds(pl.multiple_of(me * 8, 8), 8)
     recv[mine, :] = send[mine, :]
 
-    later[4].wait()
+    later[3].wait()
     pw_rows = dot(repeat16, pw[...]).astype(BF)
     kron = dot_nt(pw_rows, repeat16)
     rows_i = lax.broadcasted_iota(jnp.int32, (512, 512), 0)
@@ -277,8 +273,7 @@
     ours = pl.ds(pl.multiple_of(dp * 32, 32), 32)
     wgr[ours, :] = mb[ours, :]
 
-    for copy in later[:2]:
-        copy.wait()
+    later[0].wait()
     high, low = split(jnp.concatenate(modes, 0))
     spread = dot(jnp.concatenate([high, low], 1), spread_cot[...])
     for q in range(8):
@@ -291,19 +286,22 @@
                 wi = wv[q, :, 1024 + col : 1024 + col + 128].astype(F32)
                 for r, value in enumerate((cr * wr + ci * wi, ci * wr - cr * wi)):
                     high, low = split(value)
-                    at = 512 * q + 256 * r + 128 * g
-                    prod[32 * a : 32 * a + 32, at : at + 128] = high
-                    prod[128 + 32 * a : 160 + 32 * a, at : at + 128] = low
-    grad = dot(prod[...], sums[...])
-    grad = grad[:128] + grad[128:]
-    pieces = [
-        jnp.concatenate([grad[32 * a : 32 * a + 32, :128], grad[32 * a : 32 * a + 32, 128:]], 0)
-        for a in range(4)
-    ]
-    high, low = split(jnp.concatenate(pieces, 1))
-    back = dot(inv_x[...], jnp.concatenate([high, low, high], 0))
+                    cols = slice(128 * g, 128 * g + 128)
+                    prod[2 * q + r, 32 * a : 32 * a + 32, cols] = high
+                    prod[2 * q + r, 128 + 32 * a : 160 + 32 * a, cols] = low
+    plain, turned = [], []
+    for q in range(8):
+        re, im = [dot_nt(sums[...], prod[2 * q + r]) for r in range(2)]
+        re = re[:, :128] + re[:, 128:]
+        im = im[:, :128] + im[:, 128:]
+        plain += [re, im]
+        turned += [-im, re]
+    grad = jnp.concatenate([jnp.concatenate(plain, 0), jnp.concatenate(turned, 0)], 1)
+    high, low = split(grad)
+    back = dot_nt(inv_x[...], high)
+    back = back[:256] + back[256:] + dot_nt(inv_x[:256], low)
     for a in range(4):
-        sb[pl.ds(a, 64, stride=4), :] = back[:, 128 * a : 128 * a + 128]
+        sb[pl.ds(a, 64, stride=4), :] = back[64 * a : 64 * a + 64]
 
     sb3 = sb.reshape(64, 4, 128)
     rb3 = rb.reshape(64, 4, 128)
@@ -329,7 +327,7 @@
         send_sem=send_sem.at[1], recv_sem=recv_sem.at[1],
         device_id={"dp": lax.rem(dp + 1, DP)}, device_id_type=MESH,
     )
-    later[3].wait()
+    later[2].wait()
     dp_drain.wait_recv()
     high, low = split(wgr[...])
     pair = jnp.concatenate([high, low], 1)
@@ -350,8 +348,8 @@
         for n in range(16):
             wg_ref[q, :, 128 * n : 128 * n + 128] = wgs[pl.ds(32 * n + q, 4, stride=8), :]
 
-    inv_y_ref[...] = small[256:384, 0:192]
-    later[2].wait()
+    inv_y_ref[...] = small[192:320, 0:192]
+    later[1].wait()
     third = drain((sb, rb), pl.ds(0, 252), 2)
     third.wait_recv()
     back_ref[...] = rb[...]
@@ -364,12 +362,12 @@
 def finish_kernel(back_ref, lin, wg_ref, inv_z, inv_y, out_h, wg_h, out, sem):
     weights = pltpu.make_async_copy(wg_ref, wg_h, sem.at[4])
     weights.start()
-    odd = lax.rem(lax.broadcasted_iota(jnp.int32, (1, 128), 1), 2) == 1
+    imag = (lax.broadcasted_iota(jnp.int32, (1, 128), 1) & 8) != 0
     tops, bottoms = [], []
     for n in range(8):
         value = back_ref[pl.ds(n, 32, stride=8), :]
         tops.append(value)
-        bottoms.append(jnp.where(odd, pltpu.roll(value, 1, 1), -pltpu.roll(value, 127, 1)))
+        bottoms.append(jnp.where(imag, pltpu.roll(value, 8, 1), -pltpu.roll(value, 120, 1)))
     stacked = jnp.concatenate([jnp.concatenate(tops, 1), jnp.concatenate(bottoms, 1)], 0)
     high, low = split(stacked)
     along = dot(inv_y[...], jnp.concatenate([high, low, high], 0))
@@ -407,26 +405,25 @@
             jax.ShapeDtypeStruct((512, 1024), BF),
             jax.ShapeDtypeStruct((128, 192), BF),
         ),
-        in_specs=[hbm] * 8,
+        in_specs=[hbm] * 7,
         out_specs=(vmem,) * 5,
         scratch_shapes=[
             pltpu.VMEM((C, NY, NZ), BF),
             pltpu.VMEM((C, NY, NZ), BF),
             pltpu.VMEM((8, KX, 2 * C * C), BF),
             pltpu.VMEM((C, C), BF),
-            pltpu.VMEM((640, 256), BF),
-            pltpu.VMEM((4096, 256), BF),
+            pltpu.VMEM((1096, 256), BF),
             pltpu.VMEM((8, 256, 256), BF),
             pltpu.VMEM((4096, 128), F32),
             pltpu.VMEM((512, 128), F32),
             pltpu.VMEM((512, 128), F32),
             pltpu.VMEM((256, 128), F32),
             pltpu.VMEM((256, 128), F32),
-            pltpu.VMEM((256, 4096), BF),
+            pltpu.VMEM((16, 256, 256), BF),
             pltpu.VMEM((256, 128), F32),
             pltpu.VMEM((256, 128), F32),
             pltpu.VMEM((512, 128), F32),
-            pltpu.SemaphoreType.DMA((10,)),
+            pltpu.SemaphoreType.DMA((9,)),
             pltpu.SemaphoreType.DMA((3,)),
             pltpu.SemaphoreType.DMA((3,)),
         ],

time: 39.6 us -> 39.5 us (level)
  no operation moved by 1% of the time
where the time goes in v5:
time: 39.5 us; the launch traced here: 39.4 us
  Pallas kernels  38.7 us (98%)
  between operations  0.64 us (2%)
    pallas_call x1, Pallas kernels, on_device(): pl.pallas_call(kernel, out_shape=(jax.ShapeDtypeStruct((256, 128), F32),...  36.8 us
    pallas_call x1, Pallas kernels, on_device(): pl.pallas_call(finish_kernel, out_shape=(jax.ShapeDtypeStruct((1, 1, C, N...  1.98 us

profile of v5, /device:TPU:2, one launch (start us, length us, event | category | flops | bytes accessed | tf_op | source)
XLA Modules:
  0.0 39.4 jit_solution(7486719346778201715)
XLA Ops:
  0.6 36.8 %shard_map.86 = (f32[256,128]{1,0:T(8,128)S(1)}, f32[32,128,128]{2,1,0:T(8,128)S(1)}, f32[8,4,2048]{2,1,0:T(4,128)S(1)}, bf16[512,1024]{1,0:T(8,128)(2,1)S(1)}, bf16[128,192]{1,0:T(8,128)(2,1)S(1)}) custom-call(bf16[1,1,32,128,128]{4,3,2,1,0:T(8,128)(2,1)} %field_h.1, bf16[1,1,32,128,128]{4,3,2,1,0:T(8,128)(2,1)} %cot_h.1, bf16[8,32,2048]{2,1,0:T(8,128)(2,1)} %weight_h.1, ...), custom_call_target="tpu_custom_call" | custom-call | flops 10000000000 | bytes 10000000 | tf_op jit(solution)/shard_map/pallas_call | solution.py:399
  37.4 2.0 %shard_map.87 = (bf16[1,1,32,128,128]{4,3,2,1,0:T(8,128)(2,1)}, f32[8,4,2048]{2,1,0:T(4,128)}) custom-call(f32[256,128]{1,0:T(8,128)S(1)} %get-tuple-element.7.back_ref, f32[32,128,128]{2,1,0:T(8,128)S(1)} %get-tuple-element.8.lin, f32[8,4,2048]{2,1,0:T(4,128)S(1)} %get-tuple-element.9.wg_ref, bf16[512,1024]{1,0:T(8,128)(2,1)S(1)} %get-tuple-element.10.inv_z, ...), custom_call_target="tpu_custom_call" | custom-call | flops 1000000000 | bytes 1000000 | tf_op jit(solution)/shard_map/pallas_call | solution.py:435

commit v6 on v5

--- a/solution.py
+++ b/solution.py
@@ -126,6 +126,14 @@
     dp = lax.axis_index("dp")
     me = lax.axis_index("gx")
 
+    barrier = pltpu.get_barrier_semaphore()
+
+    @pl.loop(0, GX // 2)
+    def _(step):
+        pl.semaphore_signal(
+            barrier, inc=1, device_id={"gx": far_first(me, step)}, device_id_type=MESH
+        )
+
     loads = []
     for n, (src, dst) in enumerate(((field_h, fx), (cot_h, cx))):
         for h in range(2):
@@ -148,9 +156,7 @@
     inv_x = small.at[576:1088]
     sums = small.at[1088:1096]
 
-    barrier = pltpu.get_barrier_semaphore()
-
-    @pl.loop(0, GX - 1)
+    @pl.loop(GX // 2, GX - 1)
     def _(step):
         pl.semaphore_signal(
             barrier, inc=1, device_id={"gx": far_first(me, step)}, device_id_type=MESH
@@ -216,7 +222,7 @@
 
     pl.semaphore_wait(barrier, GX - 1 + DP - 1)
 
-    @pl.loop(0, GX - 1)
+    @pl.loop(0, GX - 1, unroll=9)
     def _(step):
         send_copy(far_first(me, step)).start()
 
@@ -316,7 +322,7 @@
             device_id_type=MESH,
         )
 
-    @pl.loop(0, GX - 1)
+    @pl.loop(0, GX - 1, unroll=9)
     def _(step):
         back_copy(far_first(me, step)).start()
 

time: 39.5 us -> 39.5 us (level)
  no operation moved by 1% of the time
where the time goes in v6:
time: 39.5 us; the launch traced here: 39.4 us
  Pallas kernels  38.7 us (98%)
  between operations  0.64 us (2%)
    pallas_call x1, Pallas kernels, on_device(): pl.pallas_call(kernel, out_shape=(jax.ShapeDtypeStruct((256, 128), F32),...  36.8 us
    pallas_call x1, Pallas kernels, on_device(): pl.pallas_call(finish_kernel, out_shape=(jax.ShapeDtypeStruct((1, 1, C, N...  1.98 us

profile of v6, /device:TPU:2, one launch (start us, length us, event | category | flops | bytes accessed | tf_op | source)
XLA Modules:
  0.0 39.4 jit_solution(5958700333494770290)
XLA Ops:
  0.6 36.8 %shard_map.86 = (f32[256,128]{1,0:T(8,128)S(1)}, f32[32,128,128]{2,1,0:T(8,128)S(1)}, f32[8,4,2048]{2,1,0:T(4,128)S(1)}, bf16[512,1024]{1,0:T(8,128)(2,1)S(1)}, bf16[128,192]{1,0:T(8,128)(2,1)S(1)}) custom-call(bf16[1,1,32,128,128]{4,3,2,1,0:T(8,128)(2,1)} %field_h.1, bf16[1,1,32,128,128]{4,3,2,1,0:T(8,128)(2,1)} %cot_h.1, bf16[8,32,2048]{2,1,0:T(8,128)(2,1)} %weight_h.1, ...), custom_call_target="tpu_custom_call" | custom-call | flops 10000000000 | bytes 10000000 | tf_op jit(solution)/shard_map/pallas_call | solution.py:405
  37.4 2.0 %shard_map.87 = (bf16[1,1,32,128,128]{4,3,2,1,0:T(8,128)(2,1)}, f32[8,4,2048]{2,1,0:T(4,128)}) custom-call(f32[256,128]{1,0:T(8,128)S(1)} %get-tuple-element.7.back_ref, f32[32,128,128]{2,1,0:T(8,128)S(1)} %get-tuple-element.8.lin, f32[8,4,2048]{2,1,0:T(4,128)S(1)} %get-tuple-element.9.wg_ref, bf16[512,1024]{1,0:T(8,128)(2,1)S(1)} %get-tuple-element.10.inv_z, ...), custom_call_target="tpu_custom_call" | custom-call | flops 1000000000 | bytes 1000000 | tf_op jit(solution)/shard_map/pallas_call | solution.py:441
